TPU v7x, 256 devices: a whole 4x4x8 slice. The times are simulated.
256 devices in a mesh: loop: 16 (over x, z_lo), rep: 16 (over z_hi, y, core).
Axes of the slice: x: 4, y: 4, z: 8 (z_hi: 2, z_lo: 4; z = z_hi * 4 + z_lo), core: 2. Of those that a mesh axis runs over, the one named last changes fastest.
Arguments:
- features: float32 [8192, 128], P('loop'), may hold values from -6 to 6
- weight: float32 [128, 256], replicated, may hold values from -0.5 to 0.5
- bias: float32 [256], replicated, may hold values from -3 to 3
- tile_values: float32 [4096, 128, 128], P(('loop', 'rep')), may hold values from -0.125 to 0.125
- tile_rows: int32 [4096], P(('loop', 'rep')), may hold values from 0 to 63, as said below
- tile_cols: int32 [4096], P(('loop', 'rep')), may hold values from 0 to 63, as said below
- tile_count: int32 [256], P(('loop', 'rep')), may hold values from 1 to 16, as said below
- cotangent: float32 [8192, 256], P('loop'), may hold values from -0.6 to 0.6
Outputs:
- output: float32 [8192, 256], P('loop')
- grad_features: float32 [8192, 128], P('loop')
- grad_weight: float32 [128, 256], replicated
- grad_bias: float32 [256], replicated
Inputs may be any that keep to these rules, and one draw needn't show every extreme that they name: `tile_rows`: every slot of a device at loop index l names a row block from l * 4 to (l + 1) * 4 - 1. `tile_cols`: for every loop index m, the live slots of one device name at most 2 different column blocks from m * 4 to (m + 1) * 4 - 1; for every loop index some device names exactly 2 of one such range. `tile_count`: for every loop index some device has all 16 slots live.
All inputs are finite; a program needn't handle non-finite values.
Results may differ from a plain program's by a relative error of at most 0.0001.
Values sent between devices are 32-bit elements; how exact they have to be, the bound alone decides.
A program may use at most 64 MiB of HBM per device.

v0:
```python
import jax
import jax.numpy as jnp
from jax import lax
from jax.sharding import PartitionSpec as P


def per_device(features, weight, bias, tile_values, tile_rows, tile_cols, tile_count, cotangent):
    highest = lax.Precision.HIGHEST
    tile_side = tile_values.shape[1]
    rows_here = features.shape[0]
    nblocks = rows_here // tile_side
    slots = tile_values.shape[0]
    local_rows = tile_rows - lax.axis_index("loop") * nblocks
    live_slot = (jnp.arange(slots, dtype=jnp.int32) < tile_count[0]).astype(jnp.float32)
    row_pick = (local_rows[:, None] == jnp.arange(nblocks, dtype=jnp.int32)[None, :]).astype(
        jnp.float32
    )
    row_pick = row_pick * live_slot[:, None]
    moved = jnp.dot(features, weight, precision=highest)
    gathered = lax.all_gather(moved, "loop", axis=0, tiled=True)
    width = gathered.shape[1]
    blocks = gathered.reshape(-1, tile_side, width)[tile_cols]
    products = jnp.einsum("kij,kjf->kif", tile_values, blocks, precision=highest)
    summed = lax.psum(
        jnp.einsum("kb,kif->bif", row_pick, products, precision=highest), "rep"
    ).reshape(rows_here, -1)
    preactive = summed + bias
    logistic = jax.nn.sigmoid(preactive)
    output = preactive * logistic
    gradient = cotangent * logistic * (1.0 + preactive * (1.0 - logistic))
    source_blocks = gradient.reshape(nblocks, tile_side, gradient.shape[1])[
        jnp.clip(local_rows, 0, nblocks - 1)
    ]
    outgoing = jnp.einsum("kji,kjf->kif", tile_values, source_blocks, precision=highest)
    outgoing = outgoing * live_slot[:, None, None]
    span = rows_here * lax.axis_size("loop") // tile_side + 2
    column_pick = (tile_cols[:, None] == jnp.arange(span, dtype=jnp.int32)[None, :]).astype(
        jnp.float32
    )
    placed = jnp.einsum("kb,kif->bif", column_pick, outgoing, precision=highest)
    placed = placed.reshape(span * tile_side, outgoing.shape[2])
    term = lax.psum_scatter(
        lax.slice_in_dim(placed, 0, rows_here * lax.axis_size("loop"), axis=0),
        "loop",
        scatter_dimension=0,
        tiled=True,
    )
    own_rows = lax.psum(term, "rep")
    weight_term = jnp.dot(features.T, own_rows, precision=highest)
    grad_rows = jnp.dot(own_rows, weight.T, precision=highest)
    bias_term = jnp.sum(gradient, axis=0)
    grad_weight, grad_bias = lax.psum((weight_term, bias_term), "loop")
    return (output, grad_rows, grad_weight, grad_bias)


def solution(mesh):
    return jax.shard_map(
        per_device,
        mesh=mesh,
        in_specs=(
            P("loop", None),
            P(),
            P(),
            P(("loop", "rep"), None, None),
            P(("loop", "rep")),
            P(("loop", "rep")),
            P(("loop", "rep")),
            P("loop", None),
        ),
        out_specs=(P("loop", None), P("loop", None), P(), P()),
        check_vma=False,
    )
```

profile of v0, /device:TPU:8, one launch (start us, length us, event | category | flops | bytes accessed | tf_op | source)
XLA Modules:
  0.0 953.2 jit_solution(14281771124516442620)
XLA Ops:
  7.2 0.0 copy-start
  7.2 0.0 all-gather.2.cloned.1.call-start
  7.2 2.4 fusion.16
  9.7 0.0 all-gather.2.cloned.1.call-update
  9.7 0.0 all-reduce.4.cloned.1.call-start
  10.4 0.7 compare_select_fusion.1
  11.1 0.7 compare_select_fusion
  11.7 189.3 %all-gather.2.cloned.1.call-done = f32[8192,256]{1,0:T(8,128)} async-done(((f32[512,256]{1,0:T(8,128)}), f32[8192,256]{1,0:T(8,128)}) %all-gather.2.cloned.1.call-update) | async-done | bytes 8388624 | tf_op jit(solution)/shard_map/all_gather | solution.py:20
  201.0 4.1 gather_fusion
  205.1 0.0 copy-done
  205.1 5.1 fusion.17
  210.2 2.2 copy.16
  212.4 0.0 copy-start.4
  212.5 0.0 copy-start.3
  212.5 1.1 fusion.2
  213.6 0.9 copy.13
  214.5 0.0 all-reduce.4.cloned.1.call-update
  214.5 0.0 reduce-scatter.2.cloned.1.call-start
  214.6 0.0 copy-done.4
  214.6 0.1 fusion.7
  214.7 168.0 %all-reduce.4.cloned.1.call-done = f32[512,256]{1,0:T(8,128)} async-done(((f32[512,256]{1,0:T(8,128)}), f32[512,256]{1,0:T(8,128)}) %all-reduce.4.cloned.1.call-update) | async-done | bytes 524304 | tf_op jit(solution)/shard_map/psum | solution.py:24
  382.6 0.0 copy-done.3
  382.6 2.2 fusion.15
  384.9 2.0 gather_fusion.1
  386.9 5.3 fusion.18
  392.2 2.2 copy.17
  394.4 5.2 fusion
  399.6 8.1 copy.14
  407.7 0.0 copy-start.1
  407.7 0.0 copy-start.2
  407.7 0.0 reduce-scatter.2.cloned.1.call-update
  407.7 0.0 all-reduce.6.cloned.1.call-start
  407.8 196.3 %reduce-scatter.2.cloned.1.call-done = f32[512,256]{1,0:T(8,128)} async-done(((f32[8192,256]{1,0:T(8,128)}), f32[512,256]{1,0:T(8,128)}) %reduce-scatter.2.cloned.1.call-update) | async-done | bytes 524304 | tf_op jit(solution)/shard_map/reduce_scatter | solution.py:42
  604.0 0.0 all-reduce.6.cloned.1.call-update
  604.1 0.0 all-reduce.8.cloned.1.call-start
  604.1 40.0 %psum.31 = f32[256]{0:T(256)} all-reduce(f32[256]{0:T(256)S(1)} %get-tuple-element.12), channel_id=1, replica_groups=mesh['loop'=16,'rep'=16] {'loop'}, use_global_device_ids=true, to_apply=%region_5.6 | all-reduce | flops 256 | bytes 2048 | tf_op jit(solution)/shard_map/psum | solution.py:52
  644.1 130.8 %all-reduce.6.cloned.1.call-done = f32[512,256]{1,0:T(8,128)} async-done(((f32[512,256]{1,0:T(8,128)}), f32[512,256]{1,0:T(8,128)}) %all-reduce.6.cloned.1.call-update) | async-done | bytes 524304 | tf_op jit(solution)/shard_map/psum | solution.py:48
  774.9 0.0 copy-done.1
  774.9 2.7 convolution_bitcast_fusion
  777.6 0.0 all-reduce.8.cloned.1.call-update
  777.6 0.0 copy-done.2
  777.6 2.3 fusion.19
  780.0 165.1 %all-reduce.8.cloned.1.call-done = f32[128,256]{0,1:T(8,128)} async-done(((f32[128,256]{0,1:T(8,128)}), f32[128,256]{0,1:T(8,128)}) %all-reduce.8.cloned.1.call-update) | async-done | bytes 131088 | tf_op jit(solution)/shard_map/psum | solution.py:52
  945.0 1.7 copy.15
  (3 shorter events, 0.0 us)
Async XLA Ops:
  7.2 198.0 %copy-start = (f32[16,128,128]{2,1,0:T(8,128)S(1)}, f32[16,128,128]{2,1,0:T(8,128)}, u32[]{:S(2)}) copy-start(f32[16,128,128]{2,1,0:T(8,128)} %param.11) | copy-start | bytes 3145732
  7.2 193.9 %all-gather.2.cloned.1.call-start = ((), (), s32[]{:S(2)}) async-start(), calls=%async_computation.1 | async-start | bytes 8912896 | tf_op jit(solution)/shard_map/all_gather | solution.py:20
  9.7 373.0 %all-reduce.4.cloned.1.call-start = ((), (), s32[]{:S(2)}) async-start(), calls=%async_computation.2 | async-start | bytes 1048576 | tf_op jit(solution)/shard_map/psum | solution.py:24
  212.4 2.1 copy-start.4
  212.5 170.2 %copy-start.3 = (f32[256]{0:T(256)S(1)}, f32[256]{0:T(256)}, u32[]{:S(2)}) copy-start(f32[256]{0:T(256)} %param.10) | copy-start | bytes 3076
  214.5 389.5 %reduce-scatter.2.cloned.1.call-start = ((), (), s32[]{:S(2)}) async-start(), calls=%async_computation.3 | async-start | bytes 8912896 | tf_op jit(solution)/shard_map/reduce_scatter | solution.py:42
  407.7 367.2 %copy-start.1 = (f32[512,128]{1,0:T(8,128)S(1)}, f32[512,128]{1,0:T(8,128)}, u32[]{:S(2)}) copy-start(f32[512,128]{1,0:T(8,128)} %param.8) | copy-start | bytes 786436
  407.7 369.9 %copy-start.2 = (f32[128,256]{1,0:T(8,128)S(1)}, f32[128,256]{1,0:T(8,128)}, u32[]{:S(2)}) copy-start(f32[128,256]{1,0:T(8,128)} %param.9) | copy-start | bytes 393220
  407.7 367.2 %all-reduce.6.cloned.1.call-start = ((), (), s32[]{:S(2)}) async-start(), calls=%async_computation.4 | async-start | bytes 1048576 | tf_op jit(solution)/shard_map/psum | solution.py:48
  604.1 341.0 %all-reduce.8.cloned.1.call-start = ((), (), s32[]{:S(2)}) async-start(), calls=%async_computation.5 | async-start | bytes 262144 | tf_op jit(solution)/shard_map/psum | solution.py:52
Sparse Core Ops, SparseCore 0:
  10.4 190.6 all-gather.1
  214.6 167.9 all-reduce.3
  407.8 196.1 reduce-scatter.1
  606.7 168.1 all-reduce.5
  777.9 167.0 all-reduce.7
where the time goes:
time: 954 us; the launch traced here: 953 us
  waiting for transfers between devices  850 us (89%)
  blocking collectives  40 us (4%)
  matrix products  24.1 us (3%)
  local copies, waits for them, and re-layouts  21.2 us (2%)
  between operations  14.5 us (2%)
    reduce_scatter x1, waiting for transfers between devices, per_device(): lax.psum_scatter(lax.slice_in_dim(placed, 0, rows_here * lax.axis_size('l...  196 us
    all_gather x1, waiting for transfers between devices, per_device(): gathered = lax.all_gather(moved, 'loop', axis=0, tiled=True)  189 us
    psum x1, waiting for transfers between devices, per_device(): lax.psum(jnp.einsum('kb,kif->bif', row_pick, products, precision=highest)...  168 us
    psum x1, waiting for transfers between devices, per_device(): grad_weight, grad_bias = lax.psum((weight_term, bias_term), 'loop')  165 us
    psum x1, waiting for transfers between devices, per_device(): own_rows = lax.psum(term, 'rep')  131 us
    psum x1, blocking collectives, per_device(): grad_weight, grad_bias = lax.psum((weight_term, bias_term), 'loop')  40 us
  transfers between devices with their start and end apart: 5, of which 5 were waited for; matrix products, arithmetic and copies ran while one was open for 0% of the time, Pallas kernels for 0%

commit v1 on v0

--- a/solution.py
+++ b/solution.py
@@ -17,7 +17,9 @@
     )
     row_pick = row_pick * live_slot[:, None]
     moved = jnp.dot(features, weight, precision=highest)
-    gathered = lax.all_gather(moved, "loop", axis=0, tiled=True)
+    gathered = jnp.concatenate(
+        lax.all_to_all(jnp.stack([moved] * lax.axis_size("loop")), "loop", 0, 0), axis=0
+    )
     width = gathered.shape[1]
     blocks = gathered.reshape(-1, tile_side, width)[tile_cols]
     products = jnp.einsum("kij,kjf->kif", tile_values, blocks, precision=highest)

time: 954 us -> 961 us (level)
    all_gather x1 -> x0, waiting for transfers between devices: 189 us -> none  [per_device(): gathered = lax.all_gather(moved, 'loop', axis=0, tiled=True)]
    all_to_all x0 -> x1, waiting for transfers between devices: none -> 185 us  [per_device(): lax.all_to_all(jnp.stack([moved] * lax.axis_size('loop')), 'loop', 0, 0)]
where the time goes in v1:
time: 961 us
  waiting for transfers between devices  847 us (88%)
  blocking collectives  40 us (4%)
  local copies, waits for them, and re-layouts  25.2 us (3%)
  matrix products  23.4 us (2%)
  between operations  14.6 us (2%)
    reduce_scatter x1, waiting for transfers between devices, per_device(): lax.psum_scatter(lax.slice_in_dim(placed, 0, rows_here * lax.axis_size('l...  196 us
    all_to_all x1, waiting for transfers between devices, per_device(): lax.all_to_all(jnp.stack([moved] * lax.axis_size('loop')), 'loop', 0, 0)  185 us
    psum x1, waiting for transfers between devices, per_device(): lax.psum(jnp.einsum('kb,kif->bif', row_pick, products, precision=highest)...  169 us
    psum x1, waiting for transfers between devices, per_device(): grad_weight, grad_bias = lax.psum((weight_term, bias_term), 'loop')  165 us
    psum x1, waiting for transfers between devices, per_device(): own_rows = lax.psum(term, 'rep')  131 us
    psum x1, blocking collectives, per_device(): grad_weight, grad_bias = lax.psum((weight_term, bias_term), 'loop')  40 us
  transfers between devices with their start and end apart: 5, of which 5 were waited for; matrix products, arithmetic and copies ran while one was open for 0% of the time, Pallas kernels for 0%

profile of v1, /device:TPU:8, one launch (start us, length us, event | category | flops | bytes accessed | tf_op | source)
XLA Modules:
  0.0 960.8 jit_solution(1751617026336383926)
XLA Ops:
  7.2 0.0 copy-start
  7.2 1.6 fusion.16
  8.8 4.0 stack.2
  12.9 0.0 copy-start.4
  12.9 0.0 copy-start.5
  12.9 8.7 all-to-all-start
  21.5 0.0 all-reduce.4.cloned.1.call-start
  22.2 0.0 copy-done.4
  22.3 0.0 copy-done.5
  22.3 185.3 %all-to-all-done = f32[16,512,256]{2,1,0:T(8,128)} async-done(((f32[16,512,256]{2,1,0:T(8,128)}), f32[16,512,256]{2,1,0:T(8,128)}, u32[]{:S(2)}, u32[]{:S(2)}) %all-to-all-start) | async-done | bytes 8388640 | tf_op jit(solution)/shard_map/all_to_all | solution.py:21
  207.6 4.1 gather_fusion
  211.7 0.0 copy-done
  211.7 5.1 fusion.17
  216.8 2.2 copy.16
  219.0 0.0 copy-start.3
  219.0 1.1 fusion.2
  220.2 0.9 copy.13
  221.0 0.0 all-reduce.4.cloned.1.call-update
  221.1 0.0 reduce-scatter.2.cloned.1.call-start
  221.1 0.1 fusion.7
  221.2 168.9 %all-reduce.4.cloned.1.call-done = f32[512,256]{1,0:T(8,128)} async-done(((f32[512,256]{1,0:T(8,128)}), f32[512,256]{1,0:T(8,128)}) %all-reduce.4.cloned.1.call-update) | async-done | bytes 524304 | tf_op jit(solution)/shard_map/psum | solution.py:26
  390.1 0.0 copy-done.3
  390.1 2.2 fusion.15
  392.3 2.0 gather_fusion.1
  394.3 5.3 fusion.18
  399.6 2.2 copy.17
  401.9 5.2 fusion
  407.1 8.1 copy.14
  415.1 0.0 copy-start.1
  415.1 0.0 copy-start.2
  415.1 0.0 reduce-scatter.2.cloned.1.call-update
  415.2 0.0 all-reduce.6.cloned.1.call-start
  415.2 196.3 %reduce-scatter.2.cloned.1.call-done = f32[512,256]{1,0:T(8,128)} async-done(((f32[8192,256]{1,0:T(8,128)}), f32[512,256]{1,0:T(8,128)}) %reduce-scatter.2.cloned.1.call-update) | async-done | bytes 524304 | tf_op jit(solution)/shard_map/reduce_scatter | solution.py:44
  611.5 0.0 all-reduce.6.cloned.1.call-update
  611.5 0.0 all-reduce.8.cloned.1.call-start
  611.6 40.0 %psum.31 = f32[256]{0:T(256)} all-reduce(f32[256]{0:T(256)S(1)} %get-tuple-element.12), channel_id=1, replica_groups=mesh['loop'=16,'rep'=16] {'loop'}, use_global_device_ids=true, to_apply=%region_5.6 | all-reduce | flops 256 | bytes 2048 | tf_op jit(solution)/shard_map/psum | solution.py:54
  651.5 131.0 %all-reduce.6.cloned.1.call-done = f32[512,256]{1,0:T(8,128)} async-done(((f32[512,256]{1,0:T(8,128)}), f32[512,256]{1,0:T(8,128)}) %all-reduce.6.cloned.1.call-update) | async-done | bytes 524304 | tf_op jit(solution)/shard_map/psum | solution.py:50
  782.5 0.0 copy-done.1
  782.5 2.7 convolution_bitcast_fusion
  785.2 0.0 all-reduce.8.cloned.1.call-update
  785.2 0.0 copy-done.2
  785.2 2.3 fusion.19
  787.5 165.1 %all-reduce.8.cloned.1.call-done = f32[128,256]{0,1:T(8,128)} async-done(((f32[128,256]{0,1:T(8,128)}), f32[128,256]{0,1:T(8,128)}) %all-reduce.8.cloned.1.call-update) | async-done | bytes 131088 | tf_op jit(solution)/shard_map/psum | solution.py:54
  952.6 1.7 copy.15
  (5 shorter events, 0.0 us)
Async XLA Ops:
  7.2 204.5 %copy-start = (f32[16,128,128]{2,1,0:T(8,128)S(1)}, f32[16,128,128]{2,1,0:T(8,128)}, u32[]{:S(2)}) copy-start(f32[16,128,128]{2,1,0:T(8,128)} %param.11) | copy-start | bytes 3145732
  12.9 9.4 copy-start.4
  12.9 9.4 copy-start.5
  12.9 194.8 %all-to-all-start = ((f32[16,512,256]{2,1,0:T(8,128)}), f32[16,512,256]{2,1,0:T(8,128)}, u32[]{:S(2)}, u32[]{:S(2)}) async-start(f32[16,512,256]{2,1,0:T(8,128)} %stack.2), calls=%async_computation | async-start | bytes 16777216 | tf_op jit(solution)/shard_map/all_to_all | solution.py:21
  21.5 368.6 %all-reduce.4.cloned.1.call-start = ((), (), s32[]{:S(2)}) async-start(), calls=%async_computation.2 | async-start | bytes 1048576 | tf_op jit(solution)/shard_map/psum | solution.py:26
  219.0 171.1 %copy-start.3 = (f32[256]{0:T(256)S(1)}, f32[256]{0:T(256)}, u32[]{:S(2)}) copy-start(f32[256]{0:T(256)} %param.10) | copy-start | bytes 3076
  221.1 390.4 %reduce-scatter.2.cloned.1.call-start = ((), (), s32[]{:S(2)}) async-start(), calls=%async_computation.3 | async-start | bytes 8912896 | tf_op jit(solution)/shard_map/reduce_scatter | solution.py:44
  415.1 367.4 %copy-start.1 = (f32[512,128]{1,0:T(8,128)S(1)}, f32[512,128]{1,0:T(8,128)}, u32[]{:S(2)}) copy-start(f32[512,128]{1,0:T(8,128)} %param.8) | copy-start | bytes 786436
  415.1 370.1 %copy-start.2 = (f32[128,256]{1,0:T(8,128)S(1)}, f32[128,256]{1,0:T(8,128)}, u32[]{:S(2)}) copy-start(f32[128,256]{1,0:T(8,128)} %param.9) | copy-start | bytes 393220
  415.2 367.3 %all-reduce.6.cloned.1.call-start = ((), (), s32[]{:S(2)}) async-start(), calls=%async_computation.4 | async-start | bytes 1048576 | tf_op jit(solution)/shard_map/psum | solution.py:50
  611.5 341.1 %all-reduce.8.cloned.1.call-start = ((), (), s32[]{:S(2)}) async-start(), calls=%async_computation.5 | async-start | bytes 262144 | tf_op jit(solution)/shard_map/psum | solution.py:54
Sparse Core Ops, SparseCore 0:
  221.2 168.8 all-reduce.3
  415.3 196.1 reduce-scatter.1
  614.3 168.1 all-reduce.5
  785.5 167.0 all-reduce.7

commit v2 on v0

--- a/solution.py
+++ b/solution.py
@@ -45,7 +45,7 @@
         scatter_dimension=0,
         tiled=True,
     )
-    own_rows = lax.psum(term, "rep")
+    own_rows = jnp.sum(lax.all_gather(term, "rep"), axis=0)
     weight_term = jnp.dot(features.T, own_rows, precision=highest)
     grad_rows = jnp.dot(own_rows, weight.T, precision=highest)
     bias_term = jnp.sum(gradient, axis=0)

time: 954 us -> 881 us (0.923)
  waiting for transfers between devices: 850 us -> 775 us
    psum x1 -> x0, waiting for transfers between devices: 131 us -> none  [per_device(): own_rows = lax.psum(term, 'rep')]
    all_gather x0 -> x1, waiting for transfers between devices: none -> 67.5 us  [per_device(): own_rows = jnp.sum(lax.all_gather(term, 'rep'), axis=0)]
    psum x1, waiting for transfers between devices: 165 us -> 153 us  [per_device(): grad_weight, grad_bias = lax.psum((weight_term, bias_term), 'loop')]
where the time goes in v2:
time: 881 us
  waiting for transfers between devices  775 us (88%)
  blocking collectives  40.7 us (5%)
  matrix products  22.1 us (3%)
  local copies, waits for them, and re-layouts  21.2 us (2%)
  between operations  14.5 us (2%)
    reduce_scatter x1, waiting for transfers between devices, per_device(): lax.psum_scatter(lax.slice_in_dim(placed, 0, rows_here * lax.axis_size('l...  196 us
    all_gather x1, waiting for transfers between devices, per_device(): gathered = lax.all_gather(moved, 'loop', axis=0, tiled=True)  189 us
    psum x1, waiting for transfers between devices, per_device(): lax.psum(jnp.einsum('kb,kif->bif', row_pick, products, precision=highest)...  168 us
    psum x1, waiting for transfers between devices, per_device(): grad_weight, grad_bias = lax.psum((weight_term, bias_term), 'loop')  153 us
    all_gather x1, waiting for transfers between devices, per_device(): own_rows = jnp.sum(lax.all_gather(term, 'rep'), axis=0)  67.5 us
    psum x1, blocking collectives, per_device(): grad_weight, grad_bias = lax.psum((weight_term, bias_term), 'loop')  40.7 us
  transfers between devices with their start and end apart: 5, of which 5 were waited for; matrix products, arithmetic and copies ran while one was open for 0% of the time, Pallas kernels for 0%

profile of v2, /device:TPU:8, one launch (start us, length us, event | category | flops | bytes accessed | tf_op | source)
XLA Modules:
  0.0 881.0 jit_solution(5528192498586917529)
XLA Ops:
  7.2 0.0 copy-start
  7.2 0.0 all-gather.4.cloned.1.call-start
  7.2 2.4 fusion.16
  9.7 0.0 all-gather.4.cloned.1.call-update
  9.7 0.0 all-reduce.3.cloned.1.call-start
  10.4 0.7 compare_select_fusion.1
  11.1 0.7 compare_select_fusion
  11.7 189.3 %all-gather.4.cloned.1.call-done = f32[8192,256]{1,0:T(8,128)} async-done(((f32[512,256]{1,0:T(8,128)}), f32[8192,256]{1,0:T(8,128)}) %all-gather.4.cloned.1.call-update) | async-done | bytes 8388624 | tf_op jit(solution)/shard_map/all_gather | solution.py:20
  201.0 4.1 gather_fusion
  205.1 0.0 copy-done
  205.1 5.1 fusion.17
  210.2 2.2 copy.16
  212.4 0.0 copy-start.4
  212.5 0.0 copy-start.3
  212.5 1.1 fusion.2
  213.6 0.9 copy.13
  214.5 0.0 all-reduce.3.cloned.1.call-update
  214.5 0.0 reduce-scatter.2.cloned.1.call-start
  214.6 0.0 copy-done.4
  214.6 0.1 fusion.7
  214.7 168.0 %all-reduce.3.cloned.1.call-done = f32[512,256]{1,0:T(8,128)} async-done(((f32[512,256]{1,0:T(8,128)}), f32[512,256]{1,0:T(8,128)}) %all-reduce.3.cloned.1.call-update) | async-done | bytes 524304 | tf_op jit(solution)/shard_map/psum | solution.py:24
  382.6 0.0 copy-done.3
  382.6 2.2 fusion.15
  384.9 2.0 gather_fusion.1
  386.9 5.3 fusion.18
  392.2 2.2 copy.17
  394.4 5.2 fusion
  399.6 8.1 copy.14
  407.7 0.0 reduce-scatter.2.cloned.1.call-update
  407.7 0.0 all-gather.6.cloned.1.call-start
  407.8 196.3 %reduce-scatter.2.cloned.1.call-done = f32[512,256]{1,0:T(8,128)} async-done(((f32[8192,256]{1,0:T(8,128)}), f32[512,256]{1,0:T(8,128)}) %reduce-scatter.2.cloned.1.call-update) | async-done | bytes 524304 | tf_op jit(solution)/shard_map/reduce_scatter | solution.py:42
  604.0 0.0 all-gather.6.cloned.1.call-update
  604.1 0.0 all-reduce.5.cloned.1.call-start
  604.1 40.7 %psum.23 = f32[256]{0:T(256)} all-reduce(f32[256]{0:T(256)S(1)} %get-tuple-element.12), channel_id=1, replica_groups=mesh['loop'=16,'rep'=16] {'loop'}, use_global_device_ids=true, to_apply=%region_5.6 | all-reduce | flops 256 | bytes 2048 | tf_op jit(solution)/shard_map/psum | solution.py:52
  644.8 67.5 %all-gather.6.cloned.1.call-done = f32[8192,256]{1,0:T(8,128)} async-done(((f32[512,256]{1,0:T(8,128)}), f32[8192,256]{1,0:T(8,128)}) %all-gather.6.cloned.1.call-update) | async-done | bytes 8388624 | tf_op jit(solution)/shard_map/all_gather | solution.py:48
  712.3 0.0 copy-start.1
  712.3 0.0 copy-start.2
  712.3 4.0 reduce_sum.18
  716.4 0.0 copy-done.1
  716.4 1.7 convolution_bitcast_fusion
  718.0 0.0 all-reduce.5.cloned.1.call-update
  718.1 0.0 copy-done.2
  718.1 1.3 fusion.19
  719.4 153.5 %all-reduce.5.cloned.1.call-done = f32[128,256]{0,1:T(8,128)} async-done(((f32[128,256]{0,1:T(8,128)}), f32[128,256]{0,1:T(8,128)}) %all-reduce.5.cloned.1.call-update) | async-done | bytes 131088 | tf_op jit(solution)/shard_map/psum | solution.py:52
  872.8 1.7 copy.15
  (3 shorter events, 0.0 us)
Async XLA Ops:
  7.2 198.0 %copy-start = (f32[16,128,128]{2,1,0:T(8,128)S(1)}, f32[16,128,128]{2,1,0:T(8,128)}, u32[]{:S(2)}) copy-start(f32[16,128,128]{2,1,0:T(8,128)} %param.11) | copy-start | bytes 3145732
  7.2 193.9 %all-gather.4.cloned.1.call-start = ((), (), s32[]{:S(2)}) async-start(), calls=%async_computation.1 | async-start | bytes 8912896 | tf_op jit(solution)/shard_map/all_gather | solution.py:20
  9.7 373.0 %all-reduce.3.cloned.1.call-start = ((), (), s32[]{:S(2)}) async-start(), calls=%async_computation.2 | async-start | bytes 1048576 | tf_op jit(solution)/shard_map/psum | solution.py:24
  212.4 2.1 copy-start.4
  212.5 170.2 %copy-start.3 = (f32[256]{0:T(256)S(1)}, f32[256]{0:T(256)}, u32[]{:S(2)}) copy-start(f32[256]{0:T(256)} %param.10) | copy-start | bytes 3076
  214.5 389.5 %reduce-scatter.2.cloned.1.call-start = ((), (), s32[]{:S(2)}) async-start(), calls=%async_computation.3 | async-start | bytes 8912896 | tf_op jit(solution)/shard_map/reduce_scatter | solution.py:42
  407.7 304.6 %all-gather.6.cloned.1.call-start = ((), (), s32[]{:S(2)}) async-start(), calls=%async_computation.5 | async-start | bytes 8912896 | tf_op jit(solution)/shard_map/all_gather | solution.py:48
  604.1 268.8 %all-reduce.5.cloned.1.call-start = ((), (), s32[]{:S(2)}) async-start(), calls=%async_computation.4 | async-start | bytes 262144 | tf_op jit(solution)/shard_map/psum | solution.py:52
  712.3 4.0 copy-start.1
  712.3 5.7 copy-start.2
Sparse Core Ops, SparseCore 0:
  10.4 190.6 all-gather.3
  214.6 167.9 all-reduce.2
  407.8 196.1 reduce-scatter.1
  607.0 105.3 all-gather.5
  718.2 154.6 all-reduce.4
